TPU v7x, 128 devices: a whole 4x4x4 slice. The times are simulated.
128 devices in a mesh: heads: 4 (over x_hi, core), cells: 32 (over z, x_lo, y).
Axes of the slice: x: 4 (x_hi: 2, x_lo: 2; x = x_hi * 2 + x_lo), y: 4, z: 4, core: 2. Of those that a mesh axis runs over, the one named last changes fastest.
Arguments:
- cells_in: bfloat16 [8, 4096, 1024], P(None, ('heads', 'cells')), may hold values from -6 to 6
- gain: float32 [1024], replicated, may hold values from 0.1 to 1.9
- w_qkv: bfloat16 [1024, 3072], replicated
- w_out: bfloat16 [1024, 1024], replicated, may hold values from -0.1875 to 0.1875
- tile_of_cell: int32 [4096], P(('heads', 'cells')), may hold values from 0 to 255
- tile_adjacent: int32 [256, 256], replicated, may hold values from 0 to 1, as said below
Outputs:
- cells_out: bfloat16 [8, 4096, 1024], P(None, ('heads', 'cells'))
Inputs may be any that keep to these rules, and one draw needn't show every extreme that they name: Tiles sit at the places of a 16 x 16 grid in an order drawn from the seed; tile_adjacent is 1 exactly where the two tiles' places differ by at most one in each grid direction, so it is symmetric with ones on the diagonal.
All inputs are finite; a program needn't handle non-finite values.
Results may differ from a plain program's by a relative error of at most 0.011.
Values may be sent and summed in bfloat16 or wider, within the bound.
A program may use at most 64 MiB of HBM per device.

v0:
```python
import math

import jax
import jax.numpy as jnp
from jax import lax
from jax.sharding import PartitionSpec as P

HEAD_DIM = 64


def tile_rows(tiles, adjacency):
    return jnp.take(adjacency, tiles, axis=0)


def start_carry(batch, rows):
    return (
        jnp.full((batch, rows), -1e30, jnp.float32),
        jnp.zeros((batch, rows), jnp.float32),
        jnp.zeros((batch, rows, HEAD_DIM), jnp.float32),
    )


def update(carry, query_matrix, rowtile, key_matrix, value_matrix, key_tiles):
    allowed = jnp.take(rowtile, key_tiles, axis=1) > 0
    logit_scores = (
        jnp.einsum("hoz,hjz->hoj", query_matrix, key_matrix, preferred_element_type=jnp.float32)
        * 0.125
    )
    masked = jnp.where(allowed[None], logit_scores, -1e30)
    running, total, summed = carry
    newest = jnp.maximum(running, jnp.max(masked, axis=-1))
    softmax_weights = jnp.where(allowed[None], jnp.exp(masked - newest[..., None]), 0.0)
    factor = jnp.exp(running - newest)
    total = total * factor + jnp.sum(softmax_weights, axis=-1)
    summed = summed * factor[..., None] + jnp.einsum(
        "ovn,onr->ovr",
        softmax_weights.astype(jnp.bfloat16),
        value_matrix,
        preferred_element_type=jnp.float32,
    )
    return (newest, total, summed)


def absorb(carry, query_matrix, rowtile, key_vals, key_tiles):
    length = key_vals.shape[1]
    step = math.gcd(length, 512)

    def one_step(index, state):
        kv_block = lax.dynamic_slice_in_dim(key_vals, index * step, step, 1)
        tile_block = lax.dynamic_slice_in_dim(key_tiles, index * step, step, 0)
        return update(
            state,
            query_matrix,
            rowtile,
            kv_block[..., :HEAD_DIM],
            kv_block[..., HEAD_DIM:],
            tile_block,
        )

    return lax.fori_loop(0, length // step, one_step, carry)


def finish(carry):
    running, total, summed = carry
    return (summed / total[..., None]).astype(jnp.bfloat16)


def on_device(cells_in, gain, w_qkv, w_out, tile_of_cell, tile_adjacent):
    genes, cell_dev, width = cells_in.shape
    groups = lax.axis_size("heads")
    group_width = width // groups
    local_heads = group_width // HEAD_DIM
    x32 = cells_in.astype(jnp.float32)
    normed = (x32 * lax.rsqrt(jnp.mean(x32 * x32, axis=-1, keepdims=True) + 1e-05) * gain).astype(
        jnp.bfloat16
    )
    projected = jnp.dot(normed, w_qkv, preferred_element_type=jnp.float32).astype(jnp.bfloat16)
    projected = projected.reshape(genes, cell_dev, 3, width)
    mixed = lax.all_to_all(projected, "heads", split_axis=3, concat_axis=1, tiled=True)
    rows_here = mixed.shape[1]
    arranged = mixed.reshape(genes, rows_here, 3, local_heads, HEAD_DIM).transpose(0, 3, 1, 2, 4)
    arranged = arranged.reshape(genes * local_heads, rows_here, 3 * HEAD_DIM)
    tiles_here = lax.all_gather(tile_of_cell, "heads", axis=0, tiled=True)
    spread = lax.all_to_all(arranged, "cells", split_axis=0, concat_axis=1, tiled=True)
    tiles_all = lax.all_gather(tiles_here, "cells", axis=0, tiled=True)
    items, total_rows = (spread.shape[0], spread.shape[1])
    block = math.gcd(total_rows, 512)
    rowtile_all = tile_rows(tiles_all, tile_adjacent)
    key_vals = spread[..., HEAD_DIM:]
    query_all = spread[..., :HEAD_DIM]

    def one_block(index):
        query_matrix = lax.dynamic_slice_in_dim(query_all, index * block, block, 1)
        rowtile = lax.dynamic_slice_in_dim(rowtile_all, index * block, block, 0)
        return finish(absorb(start_carry(items, block), query_matrix, rowtile, key_vals, tiles_all))

    blocks_out = lax.map(one_block, jnp.arange(total_rows // block, dtype=jnp.int32))
    attention_output = blocks_out.transpose(1, 0, 2, 3).reshape(
        items, total_rows // 2, 2 * HEAD_DIM
    )
    returned = lax.all_to_all(attention_output, "cells", split_axis=1, concat_axis=0, tiled=True)
    attended = returned.reshape(genes * local_heads, rows_here, HEAD_DIM)
    heads_out = (
        attended.reshape(genes, local_heads, rows_here, HEAD_DIM)
        .transpose(0, 2, 1, 3)
        .reshape(genes, rows_here, group_width)
    )
    merged = lax.all_to_all(heads_out, "heads", split_axis=1, concat_axis=2, tiled=True)
    return jnp.dot(merged, w_out, preferred_element_type=jnp.float32).astype(jnp.bfloat16)


def solution(mesh):
    return jax.shard_map(
        on_device,
        mesh=mesh,
        in_specs=(P(None, ("heads", "cells"), None), P(), P(), P(), P(("heads", "cells")), P()),
        out_specs=P(None, ("heads", "cells"), None),
        check_vma=False,
    )
```

profile of v0, /device:TPU:1, one launch (start us, length us, event | category | flops | bytes accessed | tf_op | source)
XLA Modules:
  0.0 929.3 jit_solution(234474254484213644)
XLA Ops:
  1.4 6.0 fusion.18
  7.4 5.6 reshape.87
  13.0 8.4 copy.41
  21.4 8.4 reshape.124
  29.8 5.9 all-to-all-start
  37.3 19.3 %all-reduce = s32[128]{0:T(128)S(1)} all-reduce(s32[128]{0:T(128)S(1)} %dynamic-update-slice), channel_id=1, replica_groups=mesh['heads'=4,'cells'=32] {'heads'}, use_global_device_ids=true, to_apply=%add | all-reduce | flops 128 | bytes 1024
  56.6 68.1 %all-gather = s32[32,1,128]{2,1,0:T(1,128)S(1)} all-gather(s32[1,1,128]{2,1,0:T(1,128)S(1)} %bitcast.115), channel_id=1, replica_groups=mesh['heads'=4,'cells'=32] {'cells'}, dimensions={0}, use_global_device_ids=true | all-gather | bytes 16896 | tf_op jit(solution)/shard_map/all_gather | solution.py:85
  124.7 6.4 reshape.125
  131.1 7.8 copy.55
  138.8 2.9 copy.43
  141.7 5.8 reshape.88
  147.5 5.4 copy.44
  152.9 4.9 all-to-all-start.1
  157.8 16.1 %gather_fusion.1 = s32[4096,256]{1,0:T(8,128)} fusion(s32[256,256]{1,0:T(8,128)S(1)} %copy-done.1, s32[4096]{0:T(1024)S(1)} %fusion.32), kind=kCustom, calls=%fused_computation.1 | custom fusion | bytes 8404992 | tf_op jit(solution)/shard_map/jit(_take)/gather | solution.py:12
  173.9 3.9 broadcast_select_fusion.2
  177.8 3.6 copy.45
  181.4 3.7 all_to_all.44
  188.4 656.2 %while.29 = (s32[]{:T(128)}, bf16[8,1,512,64]{2,3,1,0:T(8,128)(2,1)}, s32[8]{0:T(128)S(1)}, s32[4096,256]{1,0:T(8,128)}, bf16[1,4096,64]{1,2,0:T(8,128)(2,1)}, /...) while((s32[]{:T(128)}, ...), condition=%wide.region_6.7_spmd, body=%wide.region_1.6_spmd.sunk | while | flops 70687240 | bytes 11321882 | solution.py:97
  191.9 77.8 %while.30 = (s32[]{:T(128)}, f32[1,512]{1,0:T(1,128)S(1)}, f32[1,512]{1,0:T(1,128)S(1)}, f32[1,512,64]{1,2,0:T(8,128)S(1)}, s32[4096]{0:T(1024)S(1)}, /*index=5*...) while((s32[]{:T(128)}, f32[1,512]{1,0:T(1,128)S(1)}, ...), condition=%wide.region_5.5_spmd.clone, body=%wide.region_2.4_spmd.clone.sunk | while | flops 70621696 | bytes 8763091 | solution.py:60
  192.1 2.3 gather_fusion
  201.8 2.3 gather_fusion
  211.5 2.3 gather_fusion
  221.2 2.3 gather_fusion
  250.4 2.3 gather_fusion
  260.1 2.3 gather_fusion
  274.0 77.8 %while.30 = (s32[]{:T(128)}, f32[1,512]{1,0:T(1,128)S(1)}, f32[1,512]{1,0:T(1,128)S(1)}, f32[1,512,64]{1,2,0:T(8,128)S(1)}, s32[4096]{0:T(1024)S(1)}, /*index=5*...) while((s32[]{:T(128)}, f32[1,512]{1,0:T(1,128)S(1)}, ...), condition=%wide.region_5.5_spmd.clone, body=%wide.region_2.4_spmd.clone.sunk | while | flops 70621696 | bytes 8763091 | solution.py:60
  274.1 2.3 gather_fusion
  283.8 2.3 gather_fusion
  322.7 2.3 gather_fusion
  332.4 2.3 gather_fusion
  356.0 77.8 %while.30 = (s32[]{:T(128)}, f32[1,512]{1,0:T(1,128)S(1)}, f32[1,512]{1,0:T(1,128)S(1)}, f32[1,512,64]{1,2,0:T(8,128)S(1)}, s32[4096]{0:T(1024)S(1)}, /*index=5*...) while((s32[]{:T(128)}, f32[1,512]{1,0:T(1,128)S(1)}, ...), condition=%wide.region_5.5_spmd.clone, body=%wide.region_2.4_spmd.clone.sunk | while | flops 70621696 | bytes 8763091 | solution.py:60
  356.1 2.3 gather_fusion
  385.3 2.3 gather_fusion
  395.0 2.3 gather_fusion
  404.7 2.3 gather_fusion
  438.0 77.8 %while.30 = (s32[]{:T(128)}, f32[1,512]{1,0:T(1,128)S(1)}, f32[1,512]{1,0:T(1,128)S(1)}, f32[1,512,64]{1,2,0:T(8,128)S(1)}, s32[4096]{0:T(1024)S(1)}, /*index=5*...) while((s32[]{:T(128)}, f32[1,512]{1,0:T(1,128)S(1)}, ...), condition=%wide.region_5.5_spmd.clone, body=%wide.region_2.4_spmd.clone.sunk | while | flops 70621696 | bytes 8763091 | solution.py:60
  457.6 2.3 gather_fusion
  467.3 2.3 gather_fusion
  496.5 2.3 gather_fusion
  506.2 2.3 gather_fusion
  520.1 77.8 %while.30 = (s32[]{:T(128)}, f32[1,512]{1,0:T(1,128)S(1)}, f32[1,512]{1,0:T(1,128)S(1)}, f32[1,512,64]{1,2,0:T(8,128)S(1)}, s32[4096]{0:T(1024)S(1)}, /*index=5*...) while((s32[]{:T(128)}, f32[1,512]{1,0:T(1,128)S(1)}, ...), condition=%wide.region_5.5_spmd.clone, body=%wide.region_2.4_spmd.clone.sunk | while | flops 70621696 | bytes 8763091 | solution.py:60
  520.2 2.3 gather_fusion
  529.9 2.3 gather_fusion
  539.6 2.3 gather_fusion
  568.8 2.3 gather_fusion
  578.5 2.3 gather_fusion
  602.1 77.8 %while.30 = (s32[]{:T(128)}, f32[1,512]{1,0:T(1,128)S(1)}, f32[1,512]{1,0:T(1,128)S(1)}, f32[1,512,64]{1,2,0:T(8,128)S(1)}, s32[4096]{0:T(1024)S(1)}, /*index=5*...) while((s32[]{:T(128)}, f32[1,512]{1,0:T(1,128)S(1)}, ...), condition=%wide.region_5.5_spmd.clone, body=%wide.region_2.4_spmd.clone.sunk | while | flops 70621696 | bytes 8763091 | solution.py:60
  602.2 2.3 gather_fusion
  631.4 2.3 gather_fusion
  641.1 2.3 gather_fusion
  650.8 2.3 gather_fusion
  684.1 77.8 %while.30 = (s32[]{:T(128)}, f32[1,512]{1,0:T(1,128)S(1)}, f32[1,512]{1,0:T(1,128)S(1)}, f32[1,512,64]{1,2,0:T(8,128)S(1)}, s32[4096]{0:T(1024)S(1)}, /*index=5*...) while((s32[]{:T(128)}, f32[1,512]{1,0:T(1,128)S(1)}, ...), condition=%wide.region_5.5_spmd.clone, body=%wide.region_2.4_spmd.clone.sunk | while | flops 70621696 | bytes 8763091 | solution.py:60
  703.7 2.3 gather_fusion
  713.4 2.3 gather_fusion
  752.3 2.3 gather_fusion
  766.1 77.8 %while.30 = (s32[]{:T(128)}, f32[1,512]{1,0:T(1,128)S(1)}, f32[1,512]{1,0:T(1,128)S(1)}, f32[1,512,64]{1,2,0:T(8,128)S(1)}, s32[4096]{0:T(1024)S(1)}, /*index=5*...) while((s32[]{:T(128)}, f32[1,512]{1,0:T(1,128)S(1)}, ...), condition=%wide.region_5.5_spmd.clone, body=%wide.region_2.4_spmd.clone.sunk | while | flops 70621696 | bytes 8763091 | solution.py:60
  766.3 2.3 gather_fusion
  844.6 2.4 copy.49
  847.0 3.8 reshape_transpose.4
  851.4 12.4 %reduce.10 = bf16[2048,128]{1,0:T(8,128)(2,1)} reduce(bf16[2048,1,128]{2,1,0:T(2,128)(2,1)S(1)} %bitcast.108, bf16[]{:T(256)} %broadcast.121), dimensions={1}, to_apply=%bitcast.61.reduce_sub_computation | reduce | bytes 1048578
  864.9 16.3 %all_to_all.54 = bf16[32,2,4096]{2,1,0:T(2,128)(2,1)} all-to-all(bf16[32,2,4096]{2,1,0:T(2,128)(2,1)S(1)} %reshape.126), channel_id=1, replica_groups=mesh['heads'=4,'cells'=32] {'cells'}, dimensions={0} | all-to-all | bytes 1048576 | tf_op jit(solution)/shard_map/all_to_all | solution.py:101
  881.2 3.6 reshape.127
  884.8 9.6 %bitcast_reduce_fusion = bf16[2048,128]{1,0:T(8,128)(2,1)} fusion(bf16[2048,1,128]{2,1,0:T(2,128)(2,1)S(1)} %reshape.127), kind=kLoop, calls=%fused_computation.53 | loop fusion | bytes 1048576 | tf_op jit(solution)/shard_map/all_to_all | solution.py:101
  898.6 28.4 %all_to_all.55 = bf16[8,128,256]{2,0,1:T(8,128)(2,1)S(1)} all-to-all(bf16[8,128,256]{2,0,1:T(8,128)(2,1)S(1)} %copy.52), channel_id=1, replica_groups=mesh['heads'=4,'cells'=32] {'heads'}, dimensions={1} | all-to-all | bytes 1048576 | tf_op jit(solution)/shard_map/all_to_all | solution.py:108
  (712 shorter events, 588.6 us)
Async XLA Ops:
  0.0 927.8 %copy-start = (bf16[1024,1024]{1,0:T(8,128)(2,1)S(1)}, bf16[1024,1024]{1,0:T(8,128)(2,1)}, u32[]{:S(2)}) copy-start(bf16[1024,1024]{1,0:T(8,128)(2,1)} %param.13) | copy-start | bytes 6291460
  29.8 5.9 copy-start.3
  29.8 7.3 copy-start.2
  29.8 94.9 %all-to-all-start = ((bf16[4,2,98304]{2,1,0:T(2,128)(2,1)}), bf16[4,2,98304]{2,1,0:T(2,128)(2,1)}, u32[]{:S(2)}, u32[]{:S(2)}) async-start(bf16[4,2,98304]{2,1,0:T(2,128)(2,1)} %reshape.124), calls=%async_computation | async-start | bytes 3145728 | tf_op jit(solution)/shard_map/all_to_all | solution.py:79
  147.5 10.4 %copy-start.1 = (s32[256,256]{1,0:T(8,128)S(1)}, s32[256,256]{1,0:T(8,128)}, u32[]{:S(2)}) copy-start(s32[256,256]{1,0:T(8,128)} %param.15) | copy-start | bytes 786436
  152.9 24.9 %all-to-all-start.1 = ((bf16[32,128,192]{1,2,0:T(8,128)(2,1)}), bf16[32,128,192]{1,2,0:T(8,128)(2,1)}, u32[]{:S(2)}, u32[]{:S(2)}) async-start(bf16[32,128,192]{1,2,0:T(8,128)(2,1)} %bitcast.102), calls=%async_computation.1 | async-start | bytes 3145728 | tf_op jit(solution)/shard_map/all_to_all | solution.py:84
  185.1 2.0 slice-start
where the time goes:
time: 939 us; the launch traced here: 929 us
  local copies, waits for them, and re-layouts  277 us (29%)
  matrix products  257 us (27%)
  other arithmetic  243 us (26%)
  blocking collectives  132 us (14%)
  starting transfers between devices  10.8 us (1%)
    gather x64, local copies, waits for them, and re-layouts, update(): allowed = jnp.take(rowtile, key_tiles, axis=1) > 0  150 us
    dot_general x64, matrix products, update(): jnp.einsum('hoz,hjz->hoj', query_matrix, key_matrix, preferred_element_ty...  144 us
    reduce_sum x64, other arithmetic, update(): total = total * factor + jnp.sum(softmax_weights, axis=-1)  117 us
    dot_general x64, matrix products, update(): jnp.einsum('ovn,onr->ovr', softmax_weights.astype(jnp.bfloat16), value_ma...  105 us
    gt x64, other arithmetic, update(): allowed = jnp.take(rowtile, key_tiles, axis=1) > 0  96 us
    all_gather x1, blocking collectives, on_device(): tiles_all = lax.all_gather(tiles_here, 'cells', axis=0, tiled=True)  68.1 us
    all_to_all x1, blocking collectives, on_device(): lax.all_to_all(heads_out, 'heads', split_axis=1, concat_axis=2, tiled=True)  28.4 us
    unnamed x16, local copies, waits for them, and re-layouts  21 us
  transfers between devices with their start and end apart: 2, of which 0 were waited for; matrix products, arithmetic and copies ran while one was open for 2% of the time, Pallas kernels for 0%

commit v1 on v0

v1 whole, which is shorter than its diff:
```python
import functools
import math

import jax
import jax.numpy as jnp
from jax import lax
from jax.experimental import pallas as pl
from jax.experimental.pallas import tpu as pltpu
from jax.sharding import PartitionSpec as P

MESH = pl.DeviceIdType.MESH
HD = 64
NDEV = 128
GENES = 8
HEADS = 16
ROWS = 32
HALF = 16
LANES = 128
GROUP = 16
NGROUP = NDEV // GROUP
TILE = 8
BIG = -1e30
QSCALE = 0.125 * math.log2(math.e)


def iota(shape, dim):
    return lax.broadcasted_iota(jnp.int32, shape, dim)


def dot(a, b):
    return jnp.dot(a, b, preferred_element_type=jnp.float32)


def dot_t(a, b):
    return lax.dot_general(a, b, (((1,), (1,)), ((), ())), preferred_element_type=jnp.float32)


def grid_places(adj):
    n = adj.shape[0]
    fi = lambda shape, dim: iota(shape, dim).astype(jnp.float32)
    degree = dot(jnp.ones((8, n), jnp.bfloat16), adj)
    corner = degree == 4.0
    before = (iota((n, n), 0) < iota((n, n), 1)).astype(jnp.bfloat16)
    order = dot(corner.astype(jnp.float32).astype(jnp.bfloat16), before)
    reach = jnp.where(corner & (order == fi((8, n), 0)), 1.0, 0.0)

    def step(_, state):
        reach, dist = state
        dist = dist + (1.0 - reach)
        return jnp.minimum(dot(reach.astype(jnp.bfloat16), adj), 1.0), dist

    reach, dist = lax.fori_loop(0, 14, step, (reach, jnp.zeros((8, n), jnp.float32)))
    dist = dist + (1.0 - reach)
    d0, d1, d2, d3 = (dist[i : i + 1] for i in range(4))
    on_path = lambda d: jnp.sum(jnp.where(d0 + d == 15.0, 1.0, 0.0), axis=1, keepdims=True)
    opp1, opp2 = on_path(d1) == 16.0, on_path(d2) == 16.0
    far = jnp.where(opp1, d1, jnp.where(opp2, d2, d3))
    side = jnp.where(opp1, d2, d1)
    other = jnp.where(opp1, d3, jnp.where(opp2, d3, d2))
    near = jnp.minimum(d0, side)
    row = jnp.where(near >= 8.0, near, 15.0 - jnp.minimum(other, far))
    near = jnp.minimum(d0, other)
    col = jnp.where(near >= 8.0, near, 15.0 - jnp.minimum(side, far))
    return row, col


def kernel(
    x_hbm, gain_ref, wqkv_hbm, wout_hbm, ids_ref, adj_ref, out_ref,
    x_buf, w_buf, wo_buf, norm_buf, send_buf, recv_buf, id_send, id_recv, table_buf,
    q_buf, k_buf, v_buf, m_buf, acc_buf, osend_buf, orecv_buf, att_buf,
    x_sem, w_sem, wo_sem, send_sem, recv_sem, idsend_sem, idrecv_sem, osend_sem, orecv_sem,
):
    hi = lax.axis_index("heads")
    ci = lax.axis_index("cells")
    me = hi * 32 + ci

    def device(p):
        return (p >> 5, p & 31)

    x_copy = pltpu.make_async_copy(x_hbm, x_buf, x_sem)
    x_copy.start()
    w_copies = []
    for c in range(4):
        for part in range(3):
            cp = pltpu.make_async_copy(
                wqkv_hbm.at[:, pl.ds(part * 1024 + c * 256, 256)], w_buf.at[c * 3 + part], w_sem.at[c * 3 + part]
            )
            cp.start()
            w_copies.append(cp)
    wo_copy = pltpu.make_async_copy(wout_hbm, wo_buf, wo_sem)
    wo_copy.start()

    barrier = pltpu.get_barrier_semaphore()

    def greet(k, _):
        pl.semaphore_signal(barrier, inc=1, device_id=device((me + k) & 127), device_id_type=MESH)
        return 0

    lax.fori_loop(1, NDEV, greet, 0)

    ids = ids_ref[...].astype(jnp.float32)
    ids = jnp.concatenate([ids, ids, ids, ids], axis=1)
    lane_row = iota((1, LANES), 1)
    for v in range(4):
        id_send[v] = jnp.where((lane_row >= 32 * v) & (lane_row < 32 * v + 32), ids, 0.0)

    x_copy.wait()
    x32 = x_buf[...].reshape(GENES * ROWS, 1024).astype(jnp.float32)
    mean = jnp.mean(x32 * x32, axis=-1, keepdims=True)
    norm_buf[...] = (x32 * lax.rsqrt(mean + 1e-05) * gain_ref[...]).astype(jnp.bfloat16)

    low = iota((GENES, ROWS, LANES), 2) < HD
    low_half = iota((GENES, HALF, LANES), 2) < HD
    xn = norm_buf[...]
    for c in range(4):
        for part in range(3):
            w_copies[c * 3 + part].wait()
        q4 = dot(xn, w_buf[c * 3]) * QSCALE
        k4 = dot(xn, w_buf[c * 3 + 1])
        v4 = dot(xn, w_buf[c * 3 + 2])
        for p in range(2):
            cut = lambda a: a[:, 128 * p : 128 * p + 128]
            swap = lambda a: pltpu.roll(a, HD, axis=1).reshape(GENES, ROWS, LANES)
            as3 = lambda a: a.reshape(GENES, ROWS, LANES)
            q2, k2, v2 = cut(q4), cut(k4), cut(v4)
            qs, ks, vs = swap(q2), swap(k2), swap(v2)
            q2, k2, v2 = as3(q2), as3(k2), as3(v2)
            head = 4 * c + 2 * p
            send_buf[:, head, 0:16, :] = jnp.where(low_half, q2[:, 0:16], qs[:, 16:32]).astype(jnp.bfloat16)
            send_buf[:, head, 16:48, :] = jnp.where(low, k2, vs).astype(jnp.bfloat16)
            send_buf[:, head + 1, 0:16, :] = jnp.where(low_half, qs[:, 0:16], q2[:, 16:32]).astype(jnp.bfloat16)
            send_buf[:, head + 1, 16:48, :] = jnp.where(low, ks, v2).astype(jnp.bfloat16)

    own = pltpu.make_async_copy(send_buf.at[me >> 4, me & 15], recv_buf.at[0], recv_sem.at[0])
    own.start()
    own_id = pltpu.make_async_copy(id_send.at[0], id_recv.at[0], idrecv_sem.at[0])
    own_id.start()
    pl.semaphore_wait(barrier, NDEV - 1)

    def send(k, _):
        p = (me + k) & 127
        pltpu.make_async_remote_copy(
            src_ref=id_send.at[k & 3], dst_ref=id_recv.at[k], send_sem=idsend_sem, recv_sem=idrecv_sem.at[k >> 4],
            device_id=device(p), device_id_type=MESH,
        ).start()
        pltpu.make_async_remote_copy(
            src_ref=send_buf.at[p >> 4, p & 15], dst_ref=recv_buf.at[k], send_sem=send_sem,
            recv_sem=recv_sem.at[k >> 4], device_id=device(p), device_id_type=MESH,
        ).start()
        return 0

    lax.fori_loop(1, NDEV, send, 0)

    row, col = grid_places(adj_ref[...].astype(jnp.float32).astype(jnp.bfloat16))
    place = iota((LANES, 256), 0).astype(jnp.float32)
    table_buf[...] = jnp.where((place == row + 64.0) | (place == col + 80.0), 1.0, 0.0).astype(jnp.bfloat16)
    ia, ib = iota((LANES, LANES), 0), iota((LANES, LANES), 1)
    same_part = (ia >= 64) & (ib >= 64) & (ia < 96) & (ib < 96) & ((ia < 80) == (ib < 80))
    penalty = jnp.where(same_part & (jnp.abs(ia - ib) > 1), BIG, 0.0).astype(jnp.bfloat16)

    m_buf[...] = jnp.full(m_buf.shape, BIG, jnp.float32)
    acc_buf[...] = jnp.zeros(acc_buf.shape, jnp.float32)

    def prepare(g):
        pltpu.make_async_copy(id_recv.at[pl.ds(0, GROUP)], id_recv.at[pl.ds(0, GROUP)], idrecv_sem.at[g]).wait()
        pltpu.make_async_copy(recv_buf.at[pl.ds(0, GROUP)], recv_buf.at[pl.ds(0, GROUP)], recv_sem.at[g]).wait()
        tile_no = iota((256, LANES), 0).astype(jnp.float32)
        low4 = iota((4, ROWS, LANES), 2) < HD
        low4h = iota((4, HALF, LANES), 2) < HD
        for part in range(4):
            s = g * GROUP + 4 * part
            cell_ids = id_recv[s] + id_recv[s + 1] + id_recv[s + 2] + id_recv[s + 3]
            hot = jnp.where(tile_no == cell_ids, 1.0, 0.0).astype(jnp.bfloat16)
            codes = dot(table_buf[...], hot).T
            fines = dot(codes.astype(jnp.bfloat16), penalty).reshape(4, ROWS, LANES)
            codes = codes.reshape(4, ROWS, LANES)
            block = recv_buf[pl.ds(s, 4)].astype(jnp.float32)
            kv = block[:, 16:48]
            qq = block[:, 0:16]
            qr = pltpu.roll(qq.reshape(4 * HALF, LANES), HD, axis=1).reshape(4, HALF, LANES)
            k_buf[pl.ds(s, 4)] = jnp.where(low4, kv, codes).astype(jnp.bfloat16)
            v_buf[pl.ds(s, 4)] = jnp.where(low4, 1.0, kv).astype(jnp.bfloat16)
            q_buf[pl.ds(s, 4), 0:16] = jnp.where(low4h, qq, fines[:, 0:16]).astype(jnp.bfloat16)
            q_buf[pl.ds(s, 4), 16:32] = jnp.where(low4h, qr, fines[:, 16:32]).astype(jnp.bfloat16)

    qn, kn = TILE * ROWS, GROUP * ROWS

    def update(t, j):
        q = q_buf[pl.ds(t * TILE, TILE)].reshape(qn, LANES)
        k = k_buf[pl.ds(j * GROUP, GROUP)].reshape(kn, LANES)
        v = v_buf[pl.ds(j * GROUP, GROUP)].reshape(kn, LANES)
        s = dot_t(q, k)
        rows = pl.ds(pl.multiple_of(t * qn, qn), qn)
        m_old = m_buf[rows]
        m_new = jnp.maximum(m_old, jnp.max(s, axis=1, keepdims=True))
        m_buf[rows] = m_new
        w = jnp.exp2(s - jnp.concatenate([m_new] * (kn // LANES), axis=1)).astype(jnp.bfloat16)
        acc_buf[rows] = acc_buf[rows] * jnp.exp2(m_old - m_new) + dot(w, v)

    def finish(t):
        rows = pl.ds(pl.multiple_of(t * qn, qn), qn)
        acc = acc_buf[rows]
        swapped = pltpu.roll(acc, HD, axis=1)
        lo = iota((qn, LANES), 1) < HD
        res = jnp.where(lo, swapped, acc) / jnp.where(lo, acc, swapped)
        res = res.reshape(TILE, ROWS, LANES)
        lo = iota((TILE, HALF, LANES), 2) < HD
        osend_buf[pl.ds(t * TILE, TILE)] = jnp.where(lo, res[:, 0:16], res[:, 16:32]).astype(jnp.bfloat16)

        def give(i, _):
            k = t * TILE + i
            p = (me - k) & 127

            @pl.when(k > 0)
            def _():
                pltpu.make_async_remote_copy(
                    src_ref=osend_buf.at[k], dst_ref=orecv_buf.at[me >> 4, me & 15], send_sem=osend_sem,
                    recv_sem=orecv_sem, device_id=device(p), device_id_type=MESH,
                ).start()

            @pl.when(k == 0)
            def _():
                pltpu.make_async_copy(osend_buf.at[0], orecv_buf.at[me >> 4, me & 15], orecv_sem).start()

            return 0

        lax.fori_loop(0, TILE, give, 0)

    def group_step(g, _):
        prepare(g)

        def old(t, _):
            update(t, g)
            return 0

        lax.fori_loop(0, 2 * g, old, 0)

        def new(i, _):
            update(2 * g + (i & 1), i >> 1)
            return 0

        lax.fori_loop(0, 2 * g + 2, new, 0)
        return 0

    last = NGROUP - 1
    lax.fori_loop(0, last, group_step, 0)
    prepare(last)

    def old_last(t, _):
        update(t, last)
        finish(t)
        return 0

    lax.fori_loop(0, 2 * last, old_last, 0)

    def new_last(t, _):
        def inner(j, _):
            update(t, j)
            return 0

        lax.fori_loop(0, NGROUP, inner, 0)
        finish(t)
        return 0

    lax.fori_loop(2 * last, 2 * NGROUP, new_last, 0)

    wo_copy.wait()
    pltpu.make_async_copy(orecv_buf, orecv_buf, orecv_sem).wait()
    lo = iota((GENES, HALF, LANES), 2) < HD
    for p in range(HEADS // 2):
        even = orecv_buf[:, 2 * p].astype(jnp.float32)
        odd = orecv_buf[:, 2 * p + 1].astype(jnp.float32)
        swap = lambda a: pltpu.roll(a.reshape(GENES * HALF, LANES), HD, axis=1).reshape(GENES, HALF, LANES)
        att_buf[:, 0:16, 128 * p : 128 * p + 128] = jnp.where(lo, even, swap(odd)).astype(jnp.bfloat16)
        att_buf[:, 16:32, 128 * p : 128 * p + 128] = jnp.where(lo, swap(even), odd).astype(jnp.bfloat16)
    att = att_buf[...].reshape(GENES * ROWS, 1024)
    for c in range(4):
        part = dot(att, wo_buf[:, 256 * c : 256 * c + 256])
        out_ref[:, :, 256 * c : 256 * c + 256] = part.astype(jnp.bfloat16).reshape(GENES, ROWS, 256)

    pltpu.make_async_copy(recv_buf.at[pl.ds(0, 127)], recv_buf.at[pl.ds(0, 127)], send_sem).wait()
    pltpu.make_async_copy(id_recv.at[pl.ds(0, 127)], id_recv.at[pl.ds(0, 127)], idsend_sem).wait()
    pltpu.make_async_copy(osend_buf.at[pl.ds(0, 127)], osend_buf.at[pl.ds(0, 127)], osend_sem).wait()


def on_device(cells_in, gain, w_qkv, w_out, tile_of_cell, tile_adjacent):
    bf, f32 = jnp.bfloat16, jnp.float32
    vm = pltpu.VMEM
    hbm = pl.BlockSpec(memory_space=pl.ANY)
    vmem = pl.BlockSpec(memory_space=pltpu.VMEM)
    return pl.pallas_call(
        kernel,
        out_shape=jax.ShapeDtypeStruct(cells_in.shape, bf),
        in_specs=[hbm, vmem, hbm, hbm, vmem, vmem],
        out_specs=vmem,
        scratch_shapes=[
            vm((GENES, ROWS, 1024), bf),
            vm((12, 1024, 256), bf),
            vm((1024, 1024), bf),
            vm((GENES * ROWS, 1024), bf),
            vm((GENES, HEADS, 48, LANES), bf),
            vm((NDEV, 48, LANES), bf),
            vm((4, 1, LANES), f32),
            vm((NDEV, 1, LANES), f32),
            vm((LANES, 256), bf),
            vm((NDEV, ROWS, LANES), bf),
            vm((NDEV, ROWS, LANES), bf),
            vm((NDEV, ROWS, LANES), bf),
            vm((NDEV * ROWS, LANES), f32),
            vm((NDEV * ROWS, LANES), f32),
            vm((NDEV, HALF, LANES), bf),
            vm((GENES, HEADS, HALF, LANES), bf),
            vm((GENES, ROWS, 1024), bf),
            pltpu.SemaphoreType.DMA,
            pltpu.SemaphoreType.DMA((12,)),
            pltpu.SemaphoreType.DMA,
            pltpu.SemaphoreType.DMA,
            pltpu.SemaphoreType.DMA((NGROUP,)),
            pltpu.SemaphoreType.DMA,
            pltpu.SemaphoreType.DMA((NGROUP,)),
            pltpu.SemaphoreType.DMA,
            pltpu.SemaphoreType.DMA,
        ],
        compiler_params=pltpu.CompilerParams(
            collective_id=0, has_side_effects=True, vmem_limit_bytes=56 * 1024 * 1024
        ),
    )(cells_in, gain.reshape(1, -1), w_qkv, w_out, tile_of_cell.reshape(1, -1), tile_adjacent)


def solution(mesh):
    return jax.shard_map(
        on_device,
        mesh=mesh,
        in_specs=(P(None, ("heads", "cells"), None), P(), P(), P(), P(("heads", "cells")), P()),
        out_specs=P(None, ("heads", "cells"), None),
        check_vma=False,
    )
```

time: 939 us -> 108 us (0.12)
  the two profiles are of different devices: /device:TPU:1 before, /device:TPU:5 now
where the time goes in v1:
time: 108 us
  Pallas kernels  106 us (98%)
  local copies, waits for them, and re-layouts  1.87 us (2%)
    pallas_call x1, Pallas kernels, on_device(): pl.pallas_call(kernel, out_shape=jax.ShapeDtypeStruct(cells_in.shape, bf)...  106 us

profile of v1, /device:TPU:5, one launch (start us, length us, event | category | flops | bytes accessed | tf_op | source)
XLA Modules:
  0.0 107.6 jit_solution(5954829009538236384)
XLA Ops:
  0.0 105.7 %shard_map.64 = bf16[8,32,1024]{2,1,0:T(8,128)(2,1)} custom-call(bf16[8,32,1024]{2,1,0:T(8,128)(2,1)} %x_hbm.1, f32[1,1024]{1,0:T(1,128)} %bitcast.2, bf16[1024,3072]{1,0:T(8,128)(2,1)} %wqkv_hbm.1, bf16[1024,1024]{1,0:T(8,128)(2,1)} %wout_hbm.1, s32[1,32]{1,0:T(1,128)} %bitcast.3, s32[256,256]{1,0:T(8,128)} %adj_ref.1), custom_call_target="tpu_custom_call" | custom-call | tf_op jit(solution)/shard_map/pallas_call | solution.py:291
  105.7 1.9 %copy.8 = bf16[8,32,1024]{2,1,0:T(8,128)(2,1)} copy(bf16[8,32,1024]{2,1,0:T(8,128)(2,1)} %shard_map.64) | data formatting | bytes 1048576

commit v2 on v1

--- a/solution.py
+++ b/solution.py
@@ -18,7 +18,7 @@
 LANES = 128
 GROUP = 16
 NGROUP = NDEV // GROUP
-TILE = 8
+CELLS = GROUP * ROWS
 BIG = -1e30
 QSCALE = 0.125 * math.log2(math.e)
 
@@ -67,7 +67,7 @@
 def kernel(
     x_hbm, gain_ref, wqkv_hbm, wout_hbm, ids_ref, adj_ref, out_ref,
     x_buf, w_buf, wo_buf, norm_buf, send_buf, recv_buf, id_send, id_recv, table_buf,
-    q_buf, k_buf, v_buf, m_buf, acc_buf, osend_buf, orecv_buf, att_buf,
+    q_buf, k_buf, v_buf, s_buf, m_buf, acc_buf, osend_buf, orecv_buf, att_buf,
     x_sem, w_sem, wo_sem, send_sem, recv_sem, idsend_sem, idrecv_sem, osend_sem, orecv_sem,
 ):
     hi = lax.axis_index("heads")
@@ -179,36 +179,38 @@
             qq = block[:, 0:16]
             qr = pltpu.roll(qq.reshape(4 * HALF, LANES), HD, axis=1).reshape(4, HALF, LANES)
             k_buf[pl.ds(s, 4)] = jnp.where(low4, kv, codes).astype(jnp.bfloat16)
-            v_buf[pl.ds(s, 4)] = jnp.where(low4, 1.0, kv).astype(jnp.bfloat16)
+            v_buf[g, 0:64, 128 * part : 128 * part + 128] = kv.reshape(4 * ROWS, LANES).T[64:128].astype(jnp.bfloat16)
             q_buf[pl.ds(s, 4), 0:16] = jnp.where(low4h, qq, fines[:, 0:16]).astype(jnp.bfloat16)
             q_buf[pl.ds(s, 4), 16:32] = jnp.where(low4h, qr, fines[:, 16:32]).astype(jnp.bfloat16)
-
-    qn, kn = TILE * ROWS, GROUP * ROWS
-
-    def update(t, j):
-        q = q_buf[pl.ds(t * TILE, TILE)].reshape(qn, LANES)
-        k = k_buf[pl.ds(j * GROUP, GROUP)].reshape(kn, LANES)
-        v = v_buf[pl.ds(j * GROUP, GROUP)].reshape(kn, LANES)
-        s = dot_t(q, k)
-        rows = pl.ds(pl.multiple_of(t * qn, qn), qn)
-        m_old = m_buf[rows]
-        m_new = jnp.maximum(m_old, jnp.max(s, axis=1, keepdims=True))
-        m_buf[rows] = m_new
-        w = jnp.exp2(s - jnp.concatenate([m_new] * (kn // LANES), axis=1)).astype(jnp.bfloat16)
-        acc_buf[rows] = acc_buf[rows] * jnp.exp2(m_old - m_new) + dot(w, v)
+        v_buf[g, 64:80, :] = jnp.ones((16, CELLS), jnp.bfloat16)
+
+    def score(item, slot):
+        t, j = item
+        q = q_buf[pl.ds(t * GROUP, GROUP)].reshape(CELLS, LANES)
+        k = k_buf[pl.ds(j * GROUP, GROUP)].reshape(CELLS, LANES)
+        s_buf[slot] = dot_t(k, q)
+
+    def update(item, slot, following=None):
+        t, j = item
+        if following is not None:
+            score(following, 1 - slot)
+        s = s_buf[slot]
+        m_old = m_buf[t]
+        m_new = jnp.maximum(m_old, jnp.max(s, axis=0, keepdims=True))
+        w = jnp.exp2(s - m_new[0:1]).astype(jnp.bfloat16)
+        acc = acc_buf[t] * jnp.exp2(m_old - m_new)[0:1] + dot(v_buf[j], w)
+        m_buf[t] = m_new
+        acc_buf[t] = acc
 
     def finish(t):
-        rows = pl.ds(pl.multiple_of(t * qn, qn), qn)
-        acc = acc_buf[rows]
-        swapped = pltpu.roll(acc, HD, axis=1)
-        lo = iota((qn, LANES), 1) < HD
-        res = jnp.where(lo, swapped, acc) / jnp.where(lo, acc, swapped)
-        res = res.reshape(TILE, ROWS, LANES)
-        lo = iota((TILE, HALF, LANES), 2) < HD
-        osend_buf[pl.ds(t * TILE, TILE)] = jnp.where(lo, res[:, 0:16], res[:, 16:32]).astype(jnp.bfloat16)
+        acc = acc_buf[t]
+        res = acc[0:64] / acc[64:65]
+        res = jnp.concatenate([res, res], axis=0).T.reshape(GROUP, ROWS, LANES)
+        lo = iota((GROUP, HALF, LANES), 2) < HD
+        osend_buf[pl.ds(t * GROUP, GROUP)] = jnp.where(lo, res[:, 0:16], res[:, 16:32]).astype(jnp.bfloat16)
 
         def give(i, _):
-            k = t * TILE + i
+            k = t * GROUP + i
             p = (me - k) & 127
 
             @pl.when(k > 0)
@@ -224,45 +226,48 @@
 
             return 0
 
-        lax.fori_loop(0, TILE, give, 0)
+        lax.fori_loop(0, GROUP, give, 0)
 
     def group_step(g, _):
         prepare(g)
 
-        def old(t, _):
-            update(t, g)
+        def item(i):
+            return (jnp.where(i < g, i, g), jnp.where(i < g, g, i - g))
+
+        score(item(0), 0)
+
+        def two(i, _):
+            update(item(2 * i), 0, item(2 * i + 1))
+            update(item(2 * i + 1), 1, item(2 * i + 2))
             return 0
 
-        lax.fori_loop(0, 2 * g, old, 0)
-
-        def new(i, _):
-            update(2 * g + (i & 1), i >> 1)
-            return 0
-
-        lax.fori_loop(0, 2 * g + 2, new, 0)
+        lax.fori_loop(0, g, two, 0)
+        update((g, g), 0)
         return 0
 
     last = NGROUP - 1
     lax.fori_loop(0, last, group_step, 0)
     prepare(last)
-
-    def old_last(t, _):
-        update(t, last)
-        finish(t)
-        return 0
-
-    lax.fori_loop(0, 2 * last, old_last, 0)
-
-    def new_last(t, _):
-        def inner(j, _):
-            update(t, j)
-            return 0
-
-        lax.fori_loop(0, NGROUP, inner, 0)
-        finish(t)
-        return 0
-
-    lax.fori_loop(2 * last, 2 * NGROUP, new_last, 0)
+    score((0, last), 0)
+
+    def two_old(i, _):
+        update((2 * i, last), 0, (2 * i + 1, last))
+        finish(2 * i)
+        update((2 * i + 1, last), 1, (2 * i + 2, last))
+        finish(2 * i + 1)
+        return 0
+
+    lax.fori_loop(0, last // 2, two_old, 0)
+    update((last - 1, last), 0, (last, 0))
+    finish(last - 1)
+
+    def two_new(i, _):
+        update((last, 2 * i), 1, (last, 2 * i + 1))
+        update((last, 2 * i + 1), 0, (last, jnp.minimum(2 * i + 2, last)))
+        return 0
+
+    lax.fori_loop(0, NGROUP // 2, two_new, 0)
+    finish(last)
 
     wo_copy.wait()
     pltpu.make_async_copy(orecv_buf, orecv_buf, orecv_sem).wait()
@@ -305,9 +310,10 @@
             vm((LANES, 256), bf),
             vm((NDEV, ROWS, LANES), bf),
             vm((NDEV, ROWS, LANES), bf),
-            vm((NDEV, ROWS, LANES), bf),
-            vm((NDEV * ROWS, LANES), f32),
-            vm((NDEV * ROWS, LANES), f32),
+            vm((NGROUP, 80, CELLS), bf),
+            vm((2, CELLS, CELLS), f32),
+            vm((NGROUP, 8, CELLS), f32),
+            vm((NGROUP, 80, CELLS), f32),
             vm((NDEV, HALF, LANES), bf),
             vm((GENES, HEADS, HALF, LANES), bf),
             vm((GENES, ROWS, 1024), bf),

time: 108 us -> 72.4 us (0.67)
  Pallas kernels: 106 us -> 70.4 us
    pallas_call x1, Pallas kernels: 106 us -> 70.4 us  [on_device(): pl.pallas_call(kernel, out_shape=jax.ShapeDtypeStruct(cells_in.shape, bf)...]
where the time goes in v2:
time: 72.4 us; the launch traced here: 72.2 us
  Pallas kernels  70.4 us (97%)
  local copies, waits for them, and re-layouts  1.87 us (3%)
    pallas_call x1, Pallas kernels, on_device(): pl.pallas_call(kernel, out_shape=jax.ShapeDtypeStruct(cells_in.shape, bf)...  70.4 us
    unnamed x1, local copies, waits for them, and re-layouts  1.87 us

profile of v2, /device:TPU:5, one launch (start us, length us, event | category | flops | bytes accessed | tf_op | source)
XLA Modules:
  0.0 72.2 jit_solution(16356266904606133290)
XLA Ops:
  0.0 70.4 %shard_map.64 = bf16[8,32,1024]{2,1,0:T(8,128)(2,1)} custom-call(bf16[8,32,1024]{2,1,0:T(8,128)(2,1)} %x_hbm.1, f32[1,1024]{1,0:T(1,128)} %bitcast.2, bf16[1024,3072]{1,0:T(8,128)(2,1)} %wqkv_hbm.1, bf16[1024,1024]{1,0:T(8,128)(2,1)} %wout_hbm.1, s32[1,32]{1,0:T(1,128)} %bitcast.3, s32[256,256]{1,0:T(8,128)} %adj_ref.1), custom_call_target="tpu_custom_call" | custom-call | tf_op jit(solution)/shard_map/pallas_call | solution.py:296
  70.4 1.9 %copy.8 = bf16[8,32,1024]{2,1,0:T(8,128)(2,1)} copy(bf16[8,32,1024]{2,1,0:T(8,128)(2,1)} %shard_map.64) | data formatting | bytes 1048576

commit v3 on v2

v3 whole, which is shorter than its diff:
```python
import functools
import math

import jax
import jax.numpy as jnp
from jax import lax
from jax.experimental import pallas as pl
from jax.experimental.pallas import tpu as pltpu
from jax.sharding import PartitionSpec as P

MESH = pl.DeviceIdType.MESH
HD = 64
NDEV = 128
GENES = 8
HEADS = 16
ROWS = 32
HALF = 16
LANES = 128
GROUP = 32
NGROUP = NDEV // GROUP
FIRST, SECOND, THIRD = 16, 32, 64
STEPS = 2
PER_STEP = (NDEV - THIRD) // STEPS
CELLS = GROUP * ROWS
QT = 16
QC = QT * ROWS
NT = NDEV // QT
BIG = -1e30
QSCALE = 0.125 * math.log2(math.e)


def iota(shape, dim):
    return lax.broadcasted_iota(jnp.int32, shape, dim)


def dot(a, b):
    return jnp.dot(a, b, preferred_element_type=jnp.float32)


def dot_t(a, b):
    return lax.dot_general(a, b, (((1,), (1,)), ((), ())), preferred_element_type=jnp.float32)


def grid_places(adj):
    n = adj.shape[0]
    fi = lambda shape, dim: iota(shape, dim).astype(jnp.float32)
    degree = dot(jnp.ones((8, n), jnp.bfloat16), adj)
    corner = degree == 4.0
    before = (iota((n, n), 0) < iota((n, n), 1)).astype(jnp.bfloat16)
    order = dot(corner.astype(jnp.float32).astype(jnp.bfloat16), before)
    reach = jnp.where(corner & (order == fi((8, n), 0)), 1.0, 0.0)

    def step(_, state):
        reach, dist = state
        dist = dist + (1.0 - reach)
        return jnp.minimum(dot(reach.astype(jnp.bfloat16), adj), 1.0), dist

    dist = jnp.zeros((8, n), jnp.float32)
    for i in range(14):
        reach, dist = step(i, (reach, dist))
    dist = dist + (1.0 - reach)
    d0, d1, d2, d3 = (dist[i : i + 1] for i in range(4))
    on_path = lambda d: jnp.sum(jnp.where(d0 + d == 15.0, 1.0, 0.0), axis=1, keepdims=True)
    opp1, opp2 = on_path(d1) == 16.0, on_path(d2) == 16.0
    far = jnp.where(opp1, d1, jnp.where(opp2, d2, d3))
    side = jnp.where(opp1, d2, d1)
    other = jnp.where(opp1, d3, jnp.where(opp2, d3, d2))
    near = jnp.minimum(d0, side)
    row = jnp.where(near >= 8.0, near, 15.0 - jnp.minimum(other, far))
    near = jnp.minimum(d0, other)
    col = jnp.where(near >= 8.0, near, 15.0 - jnp.minimum(side, far))
    return row, col


def kernel(
    x_hbm, gain_ref, wqkv_hbm, ids_ref, adj_ref, att_buf,
    x_buf, w_buf, norm_buf, send_buf, recv_buf, id_near, id_send, id_recv, table_buf,
    q_buf, k_buf, v_buf, s_buf, m_buf, acc_buf, osend_buf, orecv_buf,
    x_sem, w_sem, send_sem, recv_sem, idsend_sem, idrecv_sem, osend_sem, orecv_sem,
):
    hi = lax.axis_index("heads")
    ci = lax.axis_index("cells")
    me = hi * 32 + ci

    def device(p):
        return (p >> 5, p & 31)

    z, y, x, core = ci >> 3, ci & 3, (hi & 2) | ((ci >> 2) & 1), hi & 1

    def moved(k, sign):
        dx, dy, dz = (k >> 2) & 3, k & 3, (k >> 5) + ((k >> 2) & 3) + (k & 3)
        px, py, pz = (x + sign * dx) & 3, (y + sign * dy) & 3, (z + sign * dz) & 3
        return ((px & 2) | (core ^ ((k >> 4) & 1)), pz * 8 + (px & 1) * 4 + py)

    def target(k):
        return moved(k, 1)

    def source(k):
        return moved(k, -1)

    x_copy = pltpu.make_async_copy(x_hbm, x_buf, x_sem)
    x_copy.start()
    w_copies = []
    for c in range(4):
        for part in range(3):
            cp = pltpu.make_async_copy(
                wqkv_hbm.at[:, pl.ds(part * 1024 + c * 256, 256)], w_buf.at[c * 3 + part], w_sem.at[c * 3 + part]
            )
            cp.start()
            w_copies.append(cp)

    barrier = pltpu.get_barrier_semaphore()

    def greet(k, _):
        pl.semaphore_signal(barrier, inc=1, device_id=device((me + k) & 127), device_id_type=MESH)
        return 0

    lax.fori_loop(1, NDEV, greet, 0)

    ids = ids_ref[...].astype(jnp.float32)
    id_near[hi] = jnp.concatenate([ids, jnp.zeros((1, 96), jnp.float32)], axis=1)

    x_copy.wait()
    x32 = x_buf[...].reshape(GENES * ROWS, 1024).astype(jnp.float32)
    mean = jnp.mean(x32 * x32, axis=-1, keepdims=True)
    norm_buf[...] = (x32 * lax.rsqrt(mean + 1e-05) * gain_ref[...]).astype(jnp.bfloat16)

    low = iota((GENES, ROWS, LANES), 2) < HD
    low_half = iota((GENES, HALF, LANES), 2) < HD
    xn = norm_buf[...]
    for cp in w_copies:
        cp.wait()
    row, col = grid_places(adj_ref[...].astype(jnp.float32).astype(jnp.bfloat16))
    place = iota((LANES, 256), 0).astype(jnp.float32)
    table_buf[...] = jnp.where((place == row + 64.0) | (place == col + 80.0), 1.0, 0.0).astype(jnp.bfloat16)
    for c in range(4):
        q4 = dot(xn, w_buf[c * 3]) * QSCALE
        k4 = dot(xn, w_buf[c * 3 + 1])
        v4 = dot(xn, w_buf[c * 3 + 2])
        for p in range(2):
            cut = lambda a: a[:, 128 * p : 128 * p + 128]
            swap = lambda a: pltpu.roll(a, HD, axis=1).reshape(GENES, ROWS, LANES)
            as3 = lambda a: a.reshape(GENES, ROWS, LANES)
            q2, k2, v2 = cut(q4), cut(k4), cut(v4)
            qs, ks, vs = swap(q2), swap(k2), swap(v2)
            q2, k2, v2 = as3(q2), as3(k2), as3(v2)
            head = 4 * c + 2 * p
            send_buf[:, head, 0:16, :] = jnp.where(low_half, q2[:, 0:16], qs[:, 16:32]).astype(jnp.bfloat16)
            send_buf[:, head, 16:48, :] = jnp.where(low, k2, vs).astype(jnp.bfloat16)
            send_buf[:, head + 1, 0:16, :] = jnp.where(low_half, qs[:, 0:16], q2[:, 16:32]).astype(jnp.bfloat16)
            send_buf[:, head + 1, 16:48, :] = jnp.where(low, ks, v2).astype(jnp.bfloat16)

    own = pltpu.make_async_copy(send_buf.at[me >> 4, me & 15], recv_buf.at[0], recv_sem.at[0])
    own.start()
    pl.semaphore_wait(barrier, NDEV - 1)

    def id_copy_near(k):
        return pltpu.make_async_remote_copy(
            src_ref=id_near.at[hi], dst_ref=id_near.at[hi], send_sem=idsend_sem.at[0], recv_sem=idrecv_sem.at[0],
            device_id=((hi + k) & 3, ci), device_id_type=MESH,
        )

    for k in range(1, 4):
        id_copy_near(k).start()

    def send(k, _):
        th, tc = target(k)
        pltpu.make_async_remote_copy(
            src_ref=send_buf.at[th * 2 + (tc >> 4), tc & 15], dst_ref=recv_buf.at[k], send_sem=send_sem,
            recv_sem=recv_sem.at[k >> 5], device_id=(th, tc), device_id_type=MESH,
        ).start()
        return 0

    lax.fori_loop(1, FIRST, send, 0, unroll=5)
    pltpu.make_async_copy(id_near.at[pl.ds(0, 3)], id_near.at[pl.ds(0, 3)], idsend_sem.at[0]).wait()
    pltpu.make_async_copy(id_near.at[pl.ds(0, 3)], id_near.at[pl.ds(0, 3)], idrecv_sem.at[0]).wait()
    for v in range(4):
        for h in range(4):
            row = id_near[h]
            id_send[v, h] = pltpu.roll(row, 32 * v, axis=1) if v else row
    id_recv[ci] = id_near[...]

    def send_ids(k, _):
        c = (ci + k) & 31
        pltpu.make_async_remote_copy(
            src_ref=id_send.at[k & 3], dst_ref=id_recv.at[ci], send_sem=idsend_sem.at[1], recv_sem=idrecv_sem.at[1],
            device_id=(hi, c), device_id_type=MESH,
        ).start()
        return 0

    lax.fori_loop(1, 32, send_ids, 0)
    lax.fori_loop(FIRST, SECOND, send, 0, unroll=8)

    ia, ib = iota((LANES, LANES), 0), iota((LANES, LANES), 1)
    same_part = (ia >= 64) & (ib >= 64) & (ia < 96) & (ib < 96) & ((ia < 80) == (ib < 80))
    penalty = jnp.where(same_part & (jnp.abs(ia - ib) > 1), BIG, 0.0).astype(jnp.bfloat16)

    lax.fori_loop(SECOND, THIRD, send, 0, unroll=8)
    m_buf[...] = jnp.full(m_buf.shape, BIG, jnp.float32)
    acc_buf[...] = jnp.zeros(acc_buf.shape, jnp.float32)

    pltpu.make_async_copy(id_recv.at[pl.ds(0, 31)], id_recv.at[pl.ds(0, 31)], idsend_sem.at[1]).wait()
    pltpu.make_async_copy(id_recv.at[pl.ds(0, 31)], id_recv.at[pl.ds(0, 31)], idrecv_sem.at[1]).wait()

    def code(g):
        tile_no = iota((256, LANES), 0).astype(jnp.float32)
        hots = []
        for part in range(GROUP // 4):
            cell_ids = 0.0
            for r in range(4):
                sh, sc = source(g * GROUP + 4 * part + r)
                cell_ids = cell_ids + id_recv[sc, sh]
            hots.append(jnp.where(tile_no == cell_ids, 1.0, 0.0).astype(jnp.bfloat16))
        codes = dot(table_buf[...], jnp.concatenate(hots, axis=1)).T.astype(jnp.bfloat16)
        k_buf[pl.ds(g * GROUP, GROUP)] = codes.reshape(GROUP, ROWS, LANES)
        q_buf[pl.ds(g * GROUP, GROUP)] = dot(codes, penalty).astype(jnp.bfloat16).reshape(GROUP, ROWS, LANES)
        v_buf[g, 64:80, :] = jnp.ones((16, CELLS), jnp.bfloat16)

    code(0)

    def prepare(g):
        @pl.when(g < STEPS)
        def _():
            for i in range(PER_STEP):
                send(THIRD + g * PER_STEP + i, 0)

        pltpu.make_async_copy(recv_buf.at[pl.ds(0, GROUP)], recv_buf.at[pl.ds(0, GROUP)], recv_sem.at[g]).wait()
        slots = pl.ds(g * GROUP, GROUP)
        low = iota((GROUP, ROWS, LANES), 2) < HD
        low_half = iota((GROUP, HALF, LANES), 2) < HD
        kv = recv_buf[slots, 16:48]
        qq = recv_buf[slots, 0:16]
        qr = pltpu.roll(qq.astype(jnp.float32).reshape(GROUP * HALF, LANES), HD, axis=1)
        qr = qr.astype(jnp.bfloat16).reshape(GROUP, HALF, LANES)
        v_buf[g, 0:64, :] = kv.reshape(CELLS, LANES).astype(jnp.float32).T[64:128].astype(jnp.bfloat16)
        k_buf[slots] = jnp.where(low, kv, k_buf[slots])
        q_buf[slots, 0:16] = jnp.where(low_half, qq, q_buf[slots, 0:16])
        q_buf[slots, 16:32] = jnp.where(low_half, qr, q_buf[slots, 16:32])

    def score(item, slot):
        t, j = item
        q = q_buf[pl.ds(t * QT, QT)].reshape(QC, LANES)
        k = k_buf[pl.ds(j * GROUP, GROUP)].reshape(CELLS, LANES)
        s_buf[slot] = dot_t(k, q)

    def update(item, slot, following=None):
        t, j = item
        if following is not None:
            score(following, 1 - slot)
        s = s_buf[slot]
        m_old = m_buf[t]
        m_new = jnp.maximum(m_old, jnp.max(s, axis=0, keepdims=True))
        w = jnp.exp2(s - m_new[0:1]).astype(jnp.bfloat16)
        acc = acc_buf[t] * jnp.exp2(m_old - m_new)[0:1] + dot(v_buf[j], w)
        m_buf[t] = m_new
        acc_buf[t] = acc

    def pack(t):
        acc = acc_buf[t]
        res = acc[0:64] / acc[64:65]
        res = jnp.concatenate([res, res], axis=0).T.reshape(QT, ROWS, LANES)
        lo = iota((QT, HALF, LANES), 2) < HD
        osend_buf[pl.ds(t * QT, QT)] = jnp.where(lo, res[:, 0:16], res[:, 16:32]).astype(jnp.bfloat16)

    def give(t):
        def one(k):
            pltpu.make_async_remote_copy(
                src_ref=osend_buf.at[k], dst_ref=orecv_buf.at[me >> 4, me & 15], send_sem=osend_sem,
                recv_sem=orecv_sem, device_id=source(k), device_id_type=MESH,
            ).start()

        @pl.when(t > 0)
        def _():
            one(t * QT)

        @pl.when(t == 0)
        def _():
            pltpu.make_async_copy(osend_buf.at[0], orecv_buf.at[me >> 4, me & 15], orecv_sem).start()

        for i in range(1, QT):
            one(t * QT + i)

    def group_step(g, _):
        prepare(g)

        def item(i):
            r = i - 2 * g
            return (jnp.where(r < 0, i, 2 * g + (r & 1)), jnp.where(r < 0, g, r >> 1))

        score(item(0), 0)

        def two(i, _):
            update(item(2 * i), 0, item(2 * i + 1))
            update(item(2 * i + 1), 1, item(2 * i + 2))
            return 0

        lax.fori_loop(0, 2 * g, two, 0)
        update(item(4 * g), 0, item(4 * g + 1))
        update(item(4 * g + 1), 1)
        code(g + 1)
        return 0

    last = NGROUP - 1
    lax.fori_loop(0, last, group_step, 0)
    prepare(last)
    score((0, last), 0)
    update((0, last), 0, (1, last))

    def two_old(i, _):
        update((2 * i + 1, last), 1, (2 * i + 2, last))
        pack(2 * i)
        give(2 * i)
        update((2 * i + 2, last), 0, (2 * i + 3, last))
        pack(2 * i + 1)
        give(2 * i + 1)
        return 0

    lax.fori_loop(0, last - 1, two_old, 0)
    items = [(2 * last - 1, last)] + [(t, j) for t in (2 * last, 2 * last + 1) for j in range(NGROUP)]
    done = 2 * last - 2
    for i, it in enumerate(items):
        update(it, (i + 1) & 1, items[i + 1] if i + 1 < len(items) else None)
        if it[1] == 0 or i == 0:
            pack(done)
            give(done)
            done += 1
    pack(done)
    give(done)

    pltpu.make_async_copy(orecv_buf, orecv_buf, orecv_sem).wait()
    lo = iota((GENES, HALF, LANES), 2) < HD
    for p in range(HEADS // 2):
        even = orecv_buf[:, 2 * p].astype(jnp.float32)
        odd = orecv_buf[:, 2 * p + 1].astype(jnp.float32)
        swap = lambda a: pltpu.roll(a.reshape(GENES * HALF, LANES), HD, axis=1).reshape(GENES, HALF, LANES)
        att_buf[:, 0:16, 128 * p : 128 * p + 128] = jnp.where(lo, even, swap(odd)).astype(jnp.bfloat16)
        att_buf[:, 16:32, 128 * p : 128 * p + 128] = jnp.where(lo, swap(even), odd).astype(jnp.bfloat16)
    pltpu.make_async_copy(recv_buf.at[pl.ds(0, NDEV - 1)], recv_buf.at[pl.ds(0, NDEV - 1)], send_sem).wait()
    pltpu.make_async_copy(osend_buf.at[pl.ds(0, 127)], osend_buf.at[pl.ds(0, 127)], osend_sem).wait()


def on_device(cells_in, gain, w_qkv, w_out, tile_of_cell, tile_adjacent):
    bf, f32 = jnp.bfloat16, jnp.float32
    vm = pltpu.VMEM
    hbm = pl.BlockSpec(memory_space=pl.ANY)
    vmem = pl.BlockSpec(memory_space=pltpu.VMEM)
    attended = pl.pallas_call(
        kernel,
        out_shape=jax.ShapeDtypeStruct(cells_in.shape, bf),
        in_specs=[hbm, vmem, hbm, vmem, vmem],
        out_specs=vmem,
        scratch_shapes=[
            vm((GENES, ROWS, 1024), bf),
            vm((12, 1024, 256), bf),
            vm((GENES * ROWS, 1024), bf),
            vm((GENES, HEADS, 48, LANES), bf),
            vm((NDEV, 48, LANES), bf),
            vm((4, 1, LANES), f32),
            vm((4, 4, 1, LANES), f32),
            vm((32, 4, 1, LANES), f32),
            vm((LANES, 256), bf),
            vm((NDEV, ROWS, LANES), bf),
            vm((NDEV, ROWS, LANES), bf),
            vm((NGROUP, 80, CELLS), bf),
            vm((2, CELLS, QC), f32),
            vm((NT, 8, QC), f32),
            vm((NT, 80, QC), f32),
            vm((NDEV, HALF, LANES), bf),
            vm((GENES, HEADS, HALF, LANES), bf),
            pltpu.SemaphoreType.DMA,
            pltpu.SemaphoreType.DMA((12,)),
            pltpu.SemaphoreType.DMA,
            pltpu.SemaphoreType.DMA((NGROUP,)),
            pltpu.SemaphoreType.DMA((2,)),
            pltpu.SemaphoreType.DMA((2,)),
            pltpu.SemaphoreType.DMA,
            pltpu.SemaphoreType.DMA,
        ],
        compiler_params=pltpu.CompilerParams(
            collective_id=0, has_side_effects=True, vmem_limit_bytes=56 * 1024 * 1024
        ),
    )(cells_in, gain.reshape(1, -1), w_qkv, tile_of_cell.reshape(1, -1), tile_adjacent)
    return jnp.dot(attended, w_out, preferred_element_type=jnp.float32).astype(bf)


def solution(mesh):
    return jax.shard_map(
        on_device,
        mesh=mesh,
        in_specs=(P(None, ("heads", "cells"), None), P(), P(), P(), P(("heads", "cells")), P()),
        out_specs=P(None, ("heads", "cells"), None),
        check_vma=False,
    )
```

time: 72.4 us -> 58.7 us (0.81)
  the two profiles are of different devices: /device:TPU:5 before, /device:TPU:1 now
where the time goes in v3:
time: 58.7 us; the launch traced here: 58.5 us
  Pallas kernels  56 us (95%)
  matrix products  2.55 us (4%)
    pallas_call x1, Pallas kernels, on_device(): pl.pallas_call(kernel, out_shape=jax.ShapeDtypeStruct(cells_in.shape, bf)...  56 us
    dot_general x1, matrix products, on_device(): jnp.dot(attended, w_out, preferred_element_type=jnp.float32).astype(bf)  2.55 us

profile of v3, /device:TPU:1, one launch (start us, length us, event | category | flops | bytes accessed | tf_op | source)
XLA Modules:
  0.0 58.5 jit_solution(18033000904529682221)
XLA Ops:
  0.0 0.0 copy-start
  0.0 56.0 %shard_map.64 = bf16[8,32,1024]{2,1,0:T(8,128)(2,1)} custom-call(bf16[8,32,1024]{2,1,0:T(8,128)(2,1)} %x_hbm.1, f32[1,1024]{1,0:T(1,128)} %bitcast.8, bf16[1024,3072]{1,0:T(8,128)(2,1)} %wqkv_hbm.1, s32[1,32]{1,0:T(1,128)} %bitcast.9, s32[256,256]{1,0:T(8,128)} %adj_ref.1), custom_call_target="tpu_custom_call" | custom-call | tf_op jit(solution)/shard_map/pallas_call | solution.py:347
  56.0 0.0 copy-done
  56.0 2.5 %fusion.2 = bf16[8,32,1024]{2,1,0:T(8,128)(2,1)} fusion(bf16[8,32,1024]{2,1,0:T(8,128)(2,1)} %shard_map.64, bf16[1024,1024]{1,0:T(8,128)(2,1)S(1)} %copy-done), kind=kOutput, calls=%fused_computation.2 | convolution fusion | flops 537133056 | bytes 3145728 | tf_op jit(solution)/shard_map/dot_general | solution.py:383
Async XLA Ops:
  0.0 56.0 %copy-start = (bf16[1024,1024]{1,0:T(8,128)(2,1)S(1)}, bf16[1024,1024]{1,0:T(8,128)(2,1)}, u32[]{:S(2)}) copy-start(bf16[1024,1024]{1,0:T(8,128)(2,1)} %param.9) | copy-start | bytes 6291460

commit v4 on v3

--- a/solution.py
+++ b/solution.py
@@ -87,16 +87,17 @@
 
     z, y, x, core = ci >> 3, ci & 3, (hi & 2) | ((ci >> 2) & 1), hi & 1
 
-    def moved(k, sign):
-        dx, dy, dz = (k >> 2) & 3, k & 3, (k >> 5) + ((k >> 2) & 3) + (k & 3)
-        px, py, pz = (x + sign * dx) & 3, (y + sign * dy) & 3, (z + sign * dz) & 3
-        return ((px & 2) | (core ^ ((k >> 4) & 1)), pz * 8 + (px & 1) * 4 + py)
-
-    def target(k):
-        return moved(k, 1)
-
-    def source(k):
-        return moved(k, -1)
+    def moved(k, i, sign):
+        dx, dy = i >> 2, i & 3
+        b = k >> 4
+        px, py, pz = (x + sign * dx) & 3, (y + sign * dy) & 3, (z + sign * ((b >> 1) + dx + dy)) & 3
+        return ((px & 2) | (core ^ (b & 1)), pz * 8 + (px & 1) * 4 + py)
+
+    def target(k, i):
+        return moved(k, i, 1)
+
+    def source(k, i):
+        return moved(k, i, -1)
 
     x_copy = pltpu.make_async_copy(x_hbm, x_buf, x_sem)
     x_copy.start()
@@ -163,15 +164,18 @@
     for k in range(1, 4):
         id_copy_near(k).start()
 
-    def send(k, _):
-        th, tc = target(k)
+    def send(k):
+        th, tc = target(k, k & 15)
         pltpu.make_async_remote_copy(
             src_ref=send_buf.at[th * 2 + (tc >> 4), tc & 15], dst_ref=recv_buf.at[k], send_sem=send_sem,
             recv_sem=recv_sem.at[k >> 5], device_id=(th, tc), device_id_type=MESH,
         ).start()
-        return 0
-
-    lax.fori_loop(1, FIRST, send, 0, unroll=5)
+
+    def send_range(start, stop):
+        for k in range(start, stop):
+            send(k)
+
+    send_range(1, FIRST)
     pltpu.make_async_copy(id_near.at[pl.ds(0, 3)], id_near.at[pl.ds(0, 3)], idsend_sem.at[0]).wait()
     pltpu.make_async_copy(id_near.at[pl.ds(0, 3)], id_near.at[pl.ds(0, 3)], idrecv_sem.at[0]).wait()
     for v in range(4):
@@ -189,13 +193,13 @@
         return 0
 
     lax.fori_loop(1, 32, send_ids, 0)
-    lax.fori_loop(FIRST, SECOND, send, 0, unroll=8)
+    send_range(FIRST, SECOND)
 
     ia, ib = iota((LANES, LANES), 0), iota((LANES, LANES), 1)
     same_part = (ia >= 64) & (ib >= 64) & (ia < 96) & (ib < 96) & ((ia < 80) == (ib < 80))
     penalty = jnp.where(same_part & (jnp.abs(ia - ib) > 1), BIG, 0.0).astype(jnp.bfloat16)
 
-    lax.fori_loop(SECOND, THIRD, send, 0, unroll=8)
+    send_range(SECOND, THIRD)
     m_buf[...] = jnp.full(m_buf.shape, BIG, jnp.float32)
     acc_buf[...] = jnp.zeros(acc_buf.shape, jnp.float32)
 
@@ -208,7 +212,7 @@
         for part in range(GROUP // 4):
             cell_ids = 0.0
             for r in range(4):
-                sh, sc = source(g * GROUP + 4 * part + r)
+                sh, sc = source(g * GROUP + 4 * part + r, (4 * part + r) & 15)
                 cell_ids = cell_ids + id_recv[sc, sh]
             hots.append(jnp.where(tile_no == cell_ids, 1.0, 0.0).astype(jnp.bfloat16))
         codes = dot(table_buf[...], jnp.concatenate(hots, axis=1)).T.astype(jnp.bfloat16)
@@ -219,10 +223,11 @@
     code(0)
 
     def prepare(g):
-        @pl.when(g < STEPS)
-        def _():
-            for i in range(PER_STEP):
-                send(THIRD + g * PER_STEP + i, 0)
+        for step in range(STEPS):
+
+            @pl.when(g == step)
+            def _():
+                send_range(THIRD + step * PER_STEP, THIRD + (step + 1) * PER_STEP)
 
         pltpu.make_async_copy(recv_buf.at[pl.ds(0, GROUP)], recv_buf.at[pl.ds(0, GROUP)], recv_sem.at[g]).wait()
         slots = pl.ds(g * GROUP, GROUP)
@@ -263,22 +268,23 @@
         osend_buf[pl.ds(t * QT, QT)] = jnp.where(lo, res[:, 0:16], res[:, 16:32]).astype(jnp.bfloat16)
 
     def give(t):
-        def one(k):
+        def one(i):
+            k = t * QT + i
             pltpu.make_async_remote_copy(
                 src_ref=osend_buf.at[k], dst_ref=orecv_buf.at[me >> 4, me & 15], send_sem=osend_sem,
-                recv_sem=orecv_sem, device_id=source(k), device_id_type=MESH,
+                recv_sem=orecv_sem, device_id=source(k, i), device_id_type=MESH,
             ).start()
 
         @pl.when(t > 0)
         def _():
-            one(t * QT)
+            one(0)
 
         @pl.when(t == 0)
         def _():
             pltpu.make_async_copy(osend_buf.at[0], orecv_buf.at[me >> 4, me & 15], orecv_sem).start()
 
         for i in range(1, QT):
-            one(t * QT + i)
+            one(i)
 
     def group_step(g, _):
         prepare(g)

time: 58.7 us -> 58.8 us (level)
  no operation moved by 1% of the time
where the time goes in v4:
time: 58.8 us; the launch traced here: 58.6 us
  Pallas kernels  56 us (95%)
  matrix products  2.55 us (4%)
    pallas_call x1, Pallas kernels, on_device(): pl.pallas_call(kernel, out_shape=jax.ShapeDtypeStruct(cells_in.shape, bf)...  56 us
    dot_general x1, matrix products, on_device(): jnp.dot(attended, w_out, preferred_element_type=jnp.float32).astype(bf)  2.55 us

profile of v4, /device:TPU:1, one launch (start us, length us, event | category | flops | bytes accessed | tf_op | source)
XLA Modules:
  0.0 58.6 jit_solution(18293409288582844931)
XLA Ops:
  0.0 0.0 copy-start
  0.0 56.0 %shard_map.64 = bf16[8,32,1024]{2,1,0:T(8,128)(2,1)} custom-call(bf16[8,32,1024]{2,1,0:T(8,128)(2,1)} %x_hbm.1, f32[1,1024]{1,0:T(1,128)} %bitcast.8, bf16[1024,3072]{1,0:T(8,128)(2,1)} %wqkv_hbm.1, s32[1,32]{1,0:T(1,128)} %bitcast.9, s32[256,256]{1,0:T(8,128)} %adj_ref.1), custom_call_target="tpu_custom_call" | custom-call | tf_op jit(solution)/shard_map/pallas_call | solution.py:353
  56.0 0.0 copy-done
  56.1 2.5 %fusion.2 = bf16[8,32,1024]{2,1,0:T(8,128)(2,1)} fusion(bf16[8,32,1024]{2,1,0:T(8,128)(2,1)} %shard_map.64, bf16[1024,1024]{1,0:T(8,128)(2,1)S(1)} %copy-done), kind=kOutput, calls=%fused_computation.2 | convolution fusion | flops 537133056 | bytes 3145728 | tf_op jit(solution)/shard_map/dot_general | solution.py:389
Async XLA Ops:
  0.0 56.0 %copy-start = (bf16[1024,1024]{1,0:T(8,128)(2,1)S(1)}, bf16[1024,1024]{1,0:T(8,128)(2,1)}, u32[]{:S(2)}) copy-start(bf16[1024,1024]{1,0:T(8,128)(2,1)} %param.9) | copy-start | bytes 6291460
